TPU v7x, 32 devices: a whole 2x2x4 slice. The times are simulated.
32 devices in a mesh: tok: 2 (over core), head: 4 (over y, x), exp: 4 (over z).
Axes of the slice: x: 2, y: 2, z: 4, core: 2. Of those that a mesh axis runs over, the one named last changes fastest.
Arguments:
- context: bfloat16 [4, 64, 4096], P('exp', 'tok', 'head'), may hold values from -6 to 6
- out_proj: bfloat16 [4096, 4096], P('head', 'exp'), may hold values from -0.125 to 0.125
- stream: float32 [4, 64, 4096], P('exp', 'tok', 'head'), may hold values from -75 to 75
- norm_gain: float32 [4096], replicated, may hold values from 0.1 to 1.9
- expert_ids: int32 [4, 64, 8], P('exp', 'tok'), may hold values from 0 to 31, as said below
- slot_ids: int32 [4, 64, 8], P('exp', 'tok'), may hold values from -1 to 11, as said below
- gate_probs: float32 [4, 64, 8], P('exp', 'tok'), may hold values from 0.02 to 0.3
- w_gate: bfloat16 [32, 3072, 4096], P(('tok', 'exp'), 'head'), may hold values from -0.09375 to 0.09375
- w_up: bfloat16 [32, 3072, 4096], P(('tok', 'exp'), 'head'), may hold values from -0.09375 to 0.09375
- w_down: bfloat16 [32, 3072, 4096], P(('tok', 'exp'), 'head'), may hold values from -0.15625 to 0.15625
Outputs:
- mixed: float32 [4, 64, 4096], P('exp', 'tok', 'head')
Inputs may be any that keep to these rules, and one draw needn't show every extreme that they name: `expert_ids`: each token names 8 different experts. `slot_ids`: within a block of 32 consecutive tokens of one image, the choices of one expert take slots 0, 1, 2, ... in token order until its 12 slots are full, later ones get -1; in every block some expert fills all 12 slots.
All inputs are finite; a program needn't handle non-finite values.
Results may differ from a plain program's by a relative error of at most 0.0034.
Values may be sent and summed in bfloat16 or wider, within the bound.
A program may use at most 128 MiB of HBM per device.

v0:
```python
import jax
import jax.numpy as jnp
from jax import lax
from jax.sharding import PartitionSpec as P

EXPERTS = 32
TOP = 8
CAP = 12
eps_value = 1e-05


def on_device(
    context, out_proj, stream, norm_gain, expert_ids, slot_ids, gate_probs, w_gate, w_up, w_down
):
    local_context = context[0]
    own_stream = stream[0]
    col_width = own_stream.shape[1]
    col_start = lax.axis_index("head") * col_width
    partial_value = jnp.dot(
        local_context,
        lax.all_gather(out_proj, "exp", axis=1, tiled=True),
        preferred_element_type=jnp.float32,
    )
    own_sum = lax.dynamic_slice_in_dim(partial_value, col_start, col_width, 1) + own_stream
    partial_value = lax.dynamic_update_slice_in_dim(partial_value, own_sum, col_start, 1)
    resid_full = lax.psum(partial_value, "head")
    resid_own = lax.dynamic_slice_in_dim(resid_full, col_start, col_width, 1)
    mean_sq = jnp.mean(resid_full * resid_full, axis=1, keepdims=True)
    gain_own = lax.dynamic_slice_in_dim(norm_gain, col_start, col_width, 0)
    normed_own = (resid_own * lax.rsqrt(mean_sq + eps_value) * gain_own).astype(jnp.bfloat16)
    choice_ids = expert_ids[0]
    choice_slots = slot_ids[0]
    weights = gate_probs[0]
    spill_slot = EXPERTS * CAP
    target = jnp.where(choice_slots >= 0, choice_ids * CAP + choice_slots, spill_slot)
    outgoing = (
        jnp.zeros((spill_slot + 1, col_width), jnp.bfloat16)
        .at[target.reshape(-1)]
        .set(jnp.repeat(normed_own, TOP, axis=0))
    )
    outgoing = outgoing[:spill_slot].reshape(EXPERTS, CAP, col_width)
    tok_count = lax.axis_size("tok")
    groups = tok_count * lax.axis_size("exp")
    local_experts = w_gate.shape[0]
    arrived = lax.all_to_all(outgoing, ("tok", "exp"), split_axis=0, concat_axis=0, tiled=True)
    arrived = arrived.reshape(groups, local_experts, CAP, col_width)
    piece = lax.all_gather(arrived, "head", axis=3, tiled=True)
    gate_more = jnp.einsum("slcd,lhd->slch", piece, w_gate, preferred_element_type=jnp.float32)
    up_more = jnp.einsum("slcd,lhd->slch", piece, w_up, preferred_element_type=jnp.float32)
    hidden = (jax.nn.silu(gate_more) * up_more).astype(jnp.bfloat16)
    produced = jnp.einsum(
        "slch,lhd->slcd", hidden, w_down, preferred_element_type=jnp.float32
    ).astype(jnp.bfloat16)
    widened = lax.optimization_barrier(produced).astype(jnp.float32)
    summed = lax.psum_scatter(
        widened.astype(jnp.bfloat16), "head", scatter_dimension=3, tiled=True
    ).astype(jnp.float32)
    returned_share = lax.all_to_all(
        summed.reshape(EXPERTS, CAP, col_width).astype(jnp.bfloat16),
        ("tok", "exp"),
        split_axis=0,
        concat_axis=0,
        tiled=True,
    ).astype(jnp.float32)
    lookup_share = jnp.concatenate(
        [returned_share.reshape(spill_slot, col_width), jnp.zeros((1, col_width), jnp.float32)],
        axis=0,
    )
    picked_share = lookup_share[target]
    expert_own = jnp.sum(picked_share * weights[:, :, None], axis=1)
    return (resid_own + expert_own)[None]


def solution(mesh):
    in_specs = (
        P("exp", "tok", "head"),
        P("head", "exp"),
        P("exp", "tok", "head"),
        P(),
        P("exp", "tok", None),
        P("exp", "tok", None),
        P("exp", "tok", None),
        P(("tok", "exp"), "head", None),
        P(("tok", "exp"), "head", None),
        P(("tok", "exp"), "head", None),
    )
    out_specs = P("exp", "tok", "head")
    return jax.shard_map(
        on_device, mesh=mesh, in_specs=in_specs, out_specs=out_specs, check_vma=False
    )
```

profile of v0, /device:TPU:0, one launch (start us, length us, event | category | flops | bytes accessed | tf_op | source)
XLA Modules:
  0.0 433.1 jit_solution(15233698592753137792)
XLA Ops:
  6.5 0.7 all-gather.3.cloned.1.call-update
  7.4 153.9 %all-gather.3.cloned.1.call-done = bf16[1024,4096]{1,0:T(8,128)(2,1)} async-done(((bf16[1024,1024]{1,0:T(8,128)(2,1)}), bf16[1024,4096]{1,0:T(8,128)(2,1)}) %all-gather.3.cloned.1.call-update) | async-done | bytes 8388624 | tf_op jit(solution)/shard_map/all_gather | solution.py:21
  161.3 4.9 %fusion.24 = f32[32,4096]{1,0:T(8,128)S(1)} fusion(bf16[1024,4096]{1,0:T(8,128)(2,1)} %all-gather.3.cloned.1.call-done, bf16[1,32,1024]{2,1,0:T(8,128)(2,1)S(1)} %copy-done), kind=kOutput, calls=%fused_computation.29 | convolution fusion | flops 268435456 | bytes 8978432 | tf_op jit(solution)/shard_map/dot_general | solution.py:19
  166.2 0.8 copy-done.2
  167.3 43.5 %all-reduce.3.cloned.1.call-done = f32[32,4096]{1,0:T(8,128)} async-done(((f32[32,4096]{1,0:T(8,128)}), f32[32,4096]{1,0:T(8,128)}) %all-reduce.3.cloned.1.call-update) | async-done | bytes 524304 | tf_op jit(solution)/shard_map/psum | solution.py:26
  210.8 1.2 multiply_reduce_fusion
  212.0 1.0 multiply_convert_fusion
  213.0 1.9 scatter_custom_fusion
  214.9 0.2 reshape.125
  215.1 30.6 %all_to_all.10 = bf16[32,12,1024]{2,1,0:T(8,128)(2,1)S(1)} all-to-all(bf16[32,12,1024]{2,1,0:T(8,128)(2,1)S(1)} %reshape.125), channel_id=1, replica_groups=mesh['tok'=2,'head'=4,'exp'=4] {'tok','exp'}, dimensions={0} | all-to-all | bytes 1572864 | tf_op jit(solution)/shard_map/all_to_all | solution.py:45
  245.7 1.0 copy.21
  246.8 0.2 reduce-scatter.2.cloned.1.call-start
  247.0 50.0 %all-gather.5.cloned.1.call-done = bf16[8,4,12,4096]{3,2,0,1:T(8,128)(2,1)} async-done(((bf16[8,4,12,1024]{3,2,0,1:T(8,128)(2,1)}), bf16[8,4,12,4096]{3,2,0,1:T(8,128)(2,1)}) %all-gather.5.cloned.1.call-update) | async-done | bytes 3145744 | tf_op jit(solution)/shard_map/all_gather | solution.py:47
  297.0 13.4 %fusion.4 = f32[4,8,12,768]{3,2,1,0:T(8,128)S(1)} fusion(bf16[8,4,12,4096]{3,2,0,1:T(8,128)(2,1)} %all-gather.5.cloned.1.call-done, bf16[4,768,4096]{2,1,0:T(8,128)(2,1)} %param.17), kind=kOutput, calls=%fused_computation.6 | convolution fusion | flops 2415919104 | bytes 29491200 | tf_op jit(solution)/shard_map/slcd,lhd->slch/dot_general | solution.py:48
  310.4 13.5 %fusion.12 = bf16[8,4,12,768]{3,2,0,1:T(8,128)(2,1)S(1)} fusion(f32[4,8,12,768]{3,2,1,0:T(8,128)S(1)} %fusion.4, bf16[8,4,12,4096]{3,2,0,1:T(8,128)(2,1)} %all-gather.5.cloned.1.call-done, bf16[4,768,4096]{2,1,0:T(8,128)(2,1)} %param.18), kind=kOutput, calls=%fused_computation.11 | convolution fusion | flops 2417688576 | bytes 30081024 | tf_op jit(solution)/shard_map/slcd,lhd->slch/dot_general | solution.py:49
  323.9 13.6 %fusion.9 = bf16[8,4,12,4096]{3,2,0,1:T(8,128)(2,1)} fusion(bf16[8,4,12,768]{3,2,0,1:T(8,128)(2,1)S(1)} %fusion.12, bf16[4,768,4096]{2,1,0:T(8,128)(2,1)} %param.19), kind=kOutput, calls=%fused_computation.9 | convolution fusion | flops 2417491968 | bytes 28901376 | tf_op jit(solution)/shard_map/slch,lhd->slcd/dot_general | solution.py:51
  337.5 52.7 %reduce-scatter.2.cloned.1.call-done = bf16[8,4,12,1024]{3,2,0,1:T(8,128)(2,1)} async-done(((bf16[8,4,12,4096]{3,2,0,1:T(8,128)(2,1)}), bf16[8,4,12,1024]{3,2,0,1:T(8,128)(2,1)}) %reduce-scatter.2.cloned.1.call-update) | async-done | bytes 786448 | tf_op jit(solution)/shard_map/reduce_scatter | solution.py:55
  390.2 2.3 copy.31
  392.5 4.6 %all-to-all-start.1 = ((bf16[32,12,1024]{2,1,0:T(8,128)(2,1)}), bf16[32,12,1024]{2,1,0:T(8,128)(2,1)S(1)}, u32[]{:S(2)}, u32[]{:S(2)}) async-start(bf16[32,12,1024]{2,1,0:T(8,128)(2,1)} %bitcast.14), calls=%async_computation.2 | async-start | bytes 2097152 | tf_op jit(solution)/shard_map/all_to_all | solution.py:58
  397.4 25.7 %all-to-all-done.1 = bf16[32,12,1024]{2,1,0:T(8,128)(2,1)S(1)} async-done(((bf16[32,12,1024]{2,1,0:T(8,128)(2,1)}), bf16[32,12,1024]{2,1,0:T(8,128)(2,1)S(1)}, u32[]{:S(2)}, u32[]{:S(2)}) %all-to-all-start.1) | async-done | bytes 786464 | tf_op jit(solution)/shard_map/all_to_all | solution.py:58
  423.1 0.2 reshape.127
  423.5 1.1 gather_fusion
  424.6 0.4 fusion.18
  424.9 1.6 add_bitcast_fusion
  (33 shorter events, 0.8 us)
Async XLA Ops:
  6.5 154.7 %copy-start = (bf16[1,32,1024]{2,1,0:T(8,128)(2,1)S(1)}, bf16[1,32,1024]{2,1,0:T(8,128)(2,1)}, u32[]{:S(2)}) copy-start(bf16[1,32,1024]{2,1,0:T(8,128)(2,1)} %param.10) | copy-start | bytes 196612
  6.5 154.7 %all-gather.3.cloned.1.call-start = ((), (), s32[]{:S(2)}) async-start(), calls=%async_computation.3 | async-start | bytes 10485760 | tf_op jit(solution)/shard_map/all_gather | solution.py:21
  7.3 203.5 %all-reduce.3.cloned.1.call-start = ((), (), s32[]{:S(2)}) async-start(), calls=%async_computation.4 | async-start | bytes 1048576 | tf_op jit(solution)/shard_map/psum | solution.py:26
  7.3 158.9 %copy-start.3 = (f32[1,32,1024]{2,1,0:T(8,128)S(1)}, f32[1,32,1024]{2,1,0:T(8,128)}, u32[]{:S(2)}) copy-start(f32[1,32,1024]{2,1,0:T(8,128)} %param.12) | copy-start | bytes 393220
  7.3 159.8 %copy-start.5 = (s32[1,32,8]{1,2,0:T(8,128)S(1)}, s32[1,32,8]{1,2,0:T(8,128)}, u32[]{:S(2)}) copy-start(s32[1,32,8]{1,2,0:T(8,128)} %param.15) | copy-start | bytes 3076
  7.3 159.8 %copy-start.6 = (s32[1,32,8]{1,2,0:T(8,128)S(1)}, s32[1,32,8]{1,2,0:T(8,128)}, u32[]{:S(2)}) copy-start(s32[1,32,8]{1,2,0:T(8,128)} %param.14) | copy-start | bytes 3076
  7.3 204.6 %dynamic-slice-start = ((f32[4096]{0:T(1024)}, s32[]{:T(128)}), f32[1024]{0:T(1024)S(1)}, s32[]{:S(2)}) async-start(f32[4096]{0:T(1024)} %param.13, s32[]{:T(128)} %select_n.51), calls=%async_computation.7 | async-start | bytes 8704 | tf_op jit(solution)/shard_map/dynamic_slice | solution.py:29
  166.2 0.8 copy-start.2
  167.1 129.9 %all-gather.5.cloned.1.call-start = ((), (), s32[]{:S(2)}) async-start(), calls=%async_computation.5 | async-start | bytes 5242880 | tf_op jit(solution)/shard_map/all_gather | solution.py:47
  246.8 143.4 %reduce-scatter.2.cloned.1.call-start = ((), (), s32[]{:S(2)}) async-start(), calls=%async_computation.6 | async-start | bytes 5242880 | tf_op jit(solution)/shard_map/reduce_scatter | solution.py:55
  337.5 59.8 %copy-start.4 = (f32[1,32,8]{1,2,0:T(8,128)S(1)}, f32[1,32,8]{1,2,0:T(8,128)}, u32[]{:S(2)}) copy-start(f32[1,32,8]{1,2,0:T(8,128)} %param.16) | copy-start | bytes 3076
  392.5 30.6 %all-to-all-start.1 = ((bf16[32,12,1024]{2,1,0:T(8,128)(2,1)}), bf16[32,12,1024]{2,1,0:T(8,128)(2,1)S(1)}, u32[]{:S(2)}, u32[]{:S(2)}) async-start(bf16[32,12,1024]{2,1,0:T(8,128)(2,1)} %bitcast.14), calls=%async_computation.2 | async-start | bytes 2097152 | tf_op jit(solution)/shard_map/all_to_all | solution.py:58
  423.3 3.2 copy-start.1
Sparse Core Ops, SparseCore 0:
  8.9 152.3 all-gather.2
  167.2 43.5 all-reduce.2
  246.9 50.0 all-gather.4
  337.6 52.5 reduce-scatter.1
where the time goes:
time: 433 us
  waiting for transfers between devices  327 us (76%)
  matrix products  45.4 us (10%)
  blocking collectives  30.6 us (7%)
  between operations  13.3 us (3%)
  local copies, waits for them, and re-layouts  7.94 us (2%)
  starting transfers between devices  4.91 us (1%)
  other arithmetic  4.33 us (1%)
    all_gather x1, waiting for transfers between devices, on_device(): lax.all_gather(out_proj, 'exp', axis=1, tiled=True)  154 us
    reduce_scatter x1, waiting for transfers between devices, on_device(): lax.psum_scatter(widened.astype(jnp.bfloat16), 'head', scatter_dimension=...  52.7 us
    all_gather x1, waiting for transfers between devices, on_device(): piece = lax.all_gather(arrived, 'head', axis=3, tiled=True)  50 us
    psum x1, waiting for transfers between devices, on_device(): resid_full = lax.psum(partial_value, 'head')  43.5 us
    all_to_all x1, blocking collectives, on_device(): lax.all_to_all(outgoing, ('tok', 'exp'), split_axis=0, concat_axis=0, til...  30.6 us
    all_to_all x1, waiting for transfers between devices, on_device(): lax.all_to_all(summed.reshape(EXPERTS, CAP, col_width).astype(jnp.bfloat1...  25.7 us
    dot_general x1, matrix products, on_device(): jnp.einsum('slch,lhd->slcd', hidden, w_down, preferred_element_type=jnp.f...  13.6 us
    dot_general x1, matrix products, on_device(): jnp.einsum('slcd,lhd->slch', piece, w_up, preferred_element_type=jnp.floa...  13.5 us
  transfers between devices with their start and end apart: 5, of which 5 were waited for; matrix products, arithmetic and copies ran while one was open for 0% of the time, Pallas kernels for 0%

commit v1 on v0

--- a/solution.py
+++ b/solution.py
@@ -23,7 +23,13 @@
     )
     own_sum = lax.dynamic_slice_in_dim(partial_value, col_start, col_width, 1) + own_stream
     partial_value = lax.dynamic_update_slice_in_dim(partial_value, own_sum, col_start, 1)
-    resid_full = lax.psum(partial_value, "head")
+    size = lax.axis_size("head")
+    resid_full, far = (partial_value, 1)
+    while far < size:
+        resid_full = resid_full + lax.ppermute(
+            resid_full, "head", [(i, i ^ far) for i in range(size)]
+        )
+        far = 2 * far
     resid_own = lax.dynamic_slice_in_dim(resid_full, col_start, col_width, 1)
     mean_sq = jnp.mean(resid_full * resid_full, axis=1, keepdims=True)
     gain_own = lax.dynamic_slice_in_dim(norm_gain, col_start, col_width, 0)

time: 433 us -> 412 us (0.952)
  waiting for transfers between devices: 327 us -> 308 us
    psum x1 -> x0, waiting for transfers between devices: 43.5 us -> none  [on_device(): resid_full = lax.psum(partial_value, 'head')]
    ppermute x0 -> x2, waiting for transfers between devices: none -> 23.7 us  [on_device(): lax.ppermute(resid_full, 'head', [(i, i ^ far) for i in range(size)])]
  transfers between devices with their start and end apart: 5 -> 6, of which waited for: 5 -> 6; matrix products, arithmetic and copies ran while one was open for 0% -> 0% of each run, Pallas kernels for 0% -> 0%
where the time goes in v1:
time: 412 us
  waiting for transfers between devices  308 us (75%)
  matrix products  45.4 us (11%)
  blocking collectives  28.6 us (7%)
  between operations  13.3 us (3%)
  starting transfers between devices  7.94 us (2%)
  local copies, waits for them, and re-layouts  7.16 us (2%)
    all_gather x1, waiting for transfers between devices, on_device(): lax.all_gather(out_proj, 'exp', axis=1, tiled=True)  154 us
    reduce_scatter x1, waiting for transfers between devices, on_device(): lax.psum_scatter(widened.astype(jnp.bfloat16), 'head', scatter_dimension=...  52.8 us
    all_gather x1, waiting for transfers between devices, on_device(): piece = lax.all_gather(arrived, 'head', axis=3, tiled=True)  50.9 us
    all_to_all x1, blocking collectives, on_device(): lax.all_to_all(outgoing, ('tok', 'exp'), split_axis=0, concat_axis=0, til...  28.6 us
    all_to_all x1, waiting for transfers between devices, on_device(): lax.all_to_all(summed.reshape(EXPERTS, CAP, col_width).astype(jnp.bfloat1...  25.7 us
    ppermute x2, waiting for transfers between devices, on_device(): lax.ppermute(resid_full, 'head', [(i, i ^ far) for i in range(size)])  23.7 us
    dot_general x1, matrix products, on_device(): jnp.einsum('slch,lhd->slcd', hidden, w_down, preferred_element_type=jnp.f...  13.6 us
    dot_general x1, matrix products, on_device(): jnp.einsum('slcd,lhd->slch', piece, w_up, preferred_element_type=jnp.floa...  13.5 us
  transfers between devices with their start and end apart: 6, of which 6 were waited for; matrix products, arithmetic and copies ran while one was open for 0% of the time, Pallas kernels for 0%

profile of v1, /device:TPU:0, one launch (start us, length us, event | category | flops | bytes accessed | tf_op | source)
XLA Modules:
  0.0 411.7 jit_solution(11642829825297371412)
XLA Ops:
  6.5 0.7 all-gather.3.cloned.1.call-update
  7.4 153.9 %all-gather.3.cloned.1.call-done = bf16[1024,4096]{1,0:T(8,128)(2,1)} async-done(((bf16[1024,1024]{1,0:T(8,128)(2,1)}), bf16[1024,4096]{1,0:T(8,128)(2,1)}) %all-gather.3.cloned.1.call-update) | async-done | bytes 8388624 | tf_op jit(solution)/shard_map/all_gather | solution.py:21
  161.3 4.9 %fusion.24 = f32[32,4096]{1,0:T(8,128)S(1)} fusion(bf16[1024,4096]{1,0:T(8,128)(2,1)} %all-gather.3.cloned.1.call-done, bf16[1,32,1024]{2,1,0:T(8,128)(2,1)S(1)} %copy-done), kind=kOutput, calls=%fused_computation.29 | convolution fusion | flops 268435456 | bytes 8978432 | tf_op jit(solution)/shard_map/dot_general | solution.py:19
  166.2 1.5 collective-permute-start
  167.8 12.4 %collective-permute-done = f32[32,4096]{1,0:T(8,128)S(1)} collective-permute-done((f32[32,4096]{1,0:T(8,128)S(1)}, f32[32,4096]{1,0:T(8,128)S(1)}, u32[]{:S(2)}, u32[]{:S(2)}) %collective-permute-start) | collective-permute-done | bytes 524320 | tf_op jit(solution)/shard_map/ppermute | solution.py:29
  180.2 1.5 collective-permute-start.1
  181.9 11.3 %collective-permute-done.1 = f32[32,4096]{1,0:T(8,128)S(1)} collective-permute-done((f32[32,4096]{1,0:T(8,128)S(1)}, f32[32,4096]{1,0:T(8,128)S(1)}, u32[]{:S(2)}, u32[]{:S(2)}) %collective-permute-start.1) | collective-permute-done | bytes 524320 | tf_op jit(solution)/shard_map/ppermute | solution.py:29
  193.3 0.2 multiply_reduce_fusion
  193.5 1.9 scatter_custom_fusion
  195.5 0.2 reshape.125
  195.7 28.6 %all_to_all.10 = bf16[32,12,1024]{2,1,0:T(8,128)(2,1)S(1)} all-to-all(bf16[32,12,1024]{2,1,0:T(8,128)(2,1)S(1)} %reshape.125), channel_id=1, replica_groups=mesh['tok'=2,'head'=4,'exp'=4] {'tok','exp'}, dimensions={0} | all-to-all | bytes 1572864 | tf_op jit(solution)/shard_map/all_to_all | solution.py:51
  224.3 1.0 copy.21
  225.4 0.2 reduce-scatter.2.cloned.1.call-start
  225.6 50.9 %all-gather.5.cloned.1.call-done = bf16[8,4,12,4096]{3,2,0,1:T(8,128)(2,1)} async-done(((bf16[8,4,12,1024]{3,2,0,1:T(8,128)(2,1)}), bf16[8,4,12,4096]{3,2,0,1:T(8,128)(2,1)}) %all-gather.5.cloned.1.call-update) | async-done | bytes 3145744 | tf_op jit(solution)/shard_map/all_gather | solution.py:53
  276.5 13.4 %fusion.4 = f32[4,8,12,768]{3,2,1,0:T(8,128)S(1)} fusion(bf16[8,4,12,4096]{3,2,0,1:T(8,128)(2,1)} %all-gather.5.cloned.1.call-done, bf16[4,768,4096]{2,1,0:T(8,128)(2,1)} %param.17), kind=kOutput, calls=%fused_computation.6 | convolution fusion | flops 2415919104 | bytes 29491200 | tf_op jit(solution)/shard_map/slcd,lhd->slch/dot_general | solution.py:54
  289.9 13.5 %fusion.12 = bf16[8,4,12,768]{3,2,0,1:T(8,128)(2,1)S(1)} fusion(f32[4,8,12,768]{3,2,1,0:T(8,128)S(1)} %fusion.4, bf16[8,4,12,4096]{3,2,0,1:T(8,128)(2,1)} %all-gather.5.cloned.1.call-done, bf16[4,768,4096]{2,1,0:T(8,128)(2,1)} %param.18), kind=kOutput, calls=%fused_computation.11 | convolution fusion | flops 2417688576 | bytes 30081024 | tf_op jit(solution)/shard_map/slcd,lhd->slch/dot_general | solution.py:55
  303.4 13.6 %fusion.9 = bf16[8,4,12,4096]{3,2,0,1:T(8,128)(2,1)} fusion(bf16[8,4,12,768]{3,2,0,1:T(8,128)(2,1)S(1)} %fusion.12, bf16[4,768,4096]{2,1,0:T(8,128)(2,1)} %param.19), kind=kOutput, calls=%fused_computation.9 | convolution fusion | flops 2417491968 | bytes 28901376 | tf_op jit(solution)/shard_map/slch,lhd->slcd/dot_general | solution.py:57
  317.0 52.8 %reduce-scatter.2.cloned.1.call-done = bf16[8,4,12,1024]{3,2,0,1:T(8,128)(2,1)} async-done(((bf16[8,4,12,4096]{3,2,0,1:T(8,128)(2,1)}), bf16[8,4,12,1024]{3,2,0,1:T(8,128)(2,1)}) %reduce-scatter.2.cloned.1.call-update) | async-done | bytes 786448 | tf_op jit(solution)/shard_map/reduce_scatter | solution.py:61
  369.8 2.3 copy.31
  372.1 4.6 %all-to-all-start.1 = ((bf16[32,12,1024]{2,1,0:T(8,128)(2,1)}), bf16[32,12,1024]{2,1,0:T(8,128)(2,1)S(1)}, u32[]{:S(2)}, u32[]{:S(2)}) async-start(bf16[32,12,1024]{2,1,0:T(8,128)(2,1)} %bitcast.14), calls=%async_computation.2 | async-start | bytes 2097152 | tf_op jit(solution)/shard_map/all_to_all | solution.py:64
  376.9 25.7 %all-to-all-done.1 = bf16[32,12,1024]{2,1,0:T(8,128)(2,1)S(1)} async-done(((bf16[32,12,1024]{2,1,0:T(8,128)(2,1)}), bf16[32,12,1024]{2,1,0:T(8,128)(2,1)S(1)}, u32[]{:S(2)}, u32[]{:S(2)}) %all-to-all-start.1) | async-done | bytes 786464 | tf_op jit(solution)/shard_map/all_to_all | solution.py:64
  403.0 1.1 gather_fusion
  404.1 0.4 fusion.18
  404.5 0.7 add_bitcast_fusion
  (33 shorter events, 1.1 us)
Async XLA Ops:
  6.5 154.7 %copy-start = (bf16[1,32,1024]{2,1,0:T(8,128)(2,1)S(1)}, bf16[1,32,1024]{2,1,0:T(8,128)(2,1)}, u32[]{:S(2)}) copy-start(bf16[1,32,1024]{2,1,0:T(8,128)(2,1)} %param.10) | copy-start | bytes 196612
  6.5 154.7 %all-gather.3.cloned.1.call-start = ((), (), s32[]{:S(2)}) async-start(), calls=%async_computation.3 | async-start | bytes 10485760 | tf_op jit(solution)/shard_map/all_gather | solution.py:21
  7.3 269.2 %all-gather.5.cloned.1.call-start = ((), (), s32[]{:S(2)}) async-start(), calls=%async_computation.4 | async-start | bytes 5242880 | tf_op jit(solution)/shard_map/all_gather | solution.py:53
  7.3 158.9 %copy-start.2 = (f32[1,32,1024]{2,1,0:T(8,128)S(1)}, f32[1,32,1024]{2,1,0:T(8,128)}, u32[]{:S(2)}) copy-start(f32[1,32,1024]{2,1,0:T(8,128)} %param.12) | copy-start | bytes 393220
  7.3 174.4 %copy-start.4 = (s32[1,32,8]{1,2,0:T(8,128)S(1)}, s32[1,32,8]{1,2,0:T(8,128)}, u32[]{:S(2)}) copy-start(s32[1,32,8]{1,2,0:T(8,128)} %param.15) | copy-start | bytes 3076
  7.3 174.4 %copy-start.5 = (s32[1,32,8]{1,2,0:T(8,128)S(1)}, s32[1,32,8]{1,2,0:T(8,128)}, u32[]{:S(2)}) copy-start(s32[1,32,8]{1,2,0:T(8,128)} %param.14) | copy-start | bytes 3076
  7.3 186.1 %dynamic-slice-start = ((f32[4096]{0:T(1024)}, s32[]{:T(128)}), f32[1024]{0:T(1024)S(1)}, s32[]{:S(2)}) async-start(f32[4096]{0:T(1024)} %param.13, s32[]{:T(128)} %select_n.51), calls=%async_computation.6 | async-start | bytes 8704 | tf_op jit(solution)/shard_map/dynamic_slice | solution.py:35
  166.2 13.9 %collective-permute-start = (f32[32,4096]{1,0:T(8,128)S(1)}, f32[32,4096]{1,0:T(8,128)S(1)}, u32[]{:S(2)}, u32[]{:S(2)}) collective-permute-start(f32[32,4096]{1,0:T(8,128)S(1)} %fusion.23), channel_id=1, source_target_pairs={{0,4},{4,0},{8,12},{12,8},{1,5},{5,1},{9,13},{13,9},{2,6},{6,2},{1... | collective-permute-start | bytes 1572872 | tf_op jit(solution)/shard_map/ppermute | solution.py:29
  180.2 13.0 %collective-permute-start.1 = (f32[32,4096]{1,0:T(8,128)S(1)}, f32[32,4096]{1,0:T(8,128)S(1)}, u32[]{:S(2)}, u32[]{:S(2)}) collective-permute-start(f32[32,4096]{1,0:T(8,128)S(1)} %add.85), channel_id=1, source_target_pairs={{0,8},{4,12},{8,0},{12,4},{1,9},{5,13},{9,1},{13,5},{2,10},{6,14},... | collective-permute-start | bytes 1572872 | tf_op jit(solution)/shard_map/ppermute | solution.py:29
  225.4 144.4 %reduce-scatter.2.cloned.1.call-start = ((), (), s32[]{:S(2)}) async-start(), calls=%async_computation.5 | async-start | bytes 5242880 | tf_op jit(solution)/shard_map/reduce_scatter | solution.py:61
  317.0 59.9 %copy-start.3 = (f32[1,32,8]{1,2,0:T(8,128)S(1)}, f32[1,32,8]{1,2,0:T(8,128)}, u32[]{:S(2)}) copy-start(f32[1,32,8]{1,2,0:T(8,128)} %param.16) | copy-start | bytes 3076
  372.1 30.6 %all-to-all-start.1 = ((bf16[32,12,1024]{2,1,0:T(8,128)(2,1)}), bf16[32,12,1024]{2,1,0:T(8,128)(2,1)S(1)}, u32[]{:S(2)}, u32[]{:S(2)}) async-start(bf16[32,12,1024]{2,1,0:T(8,128)(2,1)} %bitcast.14), calls=%async_computation.2 | async-start | bytes 2097152 | tf_op jit(solution)/shard_map/all_to_all | solution.py:64
  402.8 2.3 copy-start.1
Sparse Core Ops, SparseCore 0:
  8.9 152.3 all-gather.2
  225.5 50.9 all-gather.4
  317.1 52.5 reduce-scatter.1
